TPU v7x, 32 devices: a whole 2x2x4 slice. The times are simulated.
32 devices in a mesh: blk: 16 (over z, y, x), grp: 2 (over core).
Axes of the slice: x: 2, y: 2, z: 4, core: 2. Of those that a mesh axis runs over, the one named last changes fastest.
Arguments:
- item_start: bfloat16 [4096, 128], P(('blk', 'grp')), may hold values from -0.5 to 0.5
- ratings: bfloat16 [4, 1024, 256], P(None, 'blk', 'grp'), may hold values from -6 to 6
- rating_bits: int32 [4, 1024], P(None, 'blk'), may hold values from -2147483648 to 2147483647, as said below
- plan: int32 [4], replicated, may hold values from 1 to 15, as said below
Outputs:
- user_factors: bfloat16 [1024, 128], P(('blk', 'grp'))
- item_factors: bfloat16 [4096, 128], P(('blk', 'grp'))
Inputs may be any that keep to these rules, and one draw needn't show every extreme that they name: `plan`: the 4 offsets are distinct, and among them are 15 and 8. `rating_bits`: every word has a set bit among bits 0 to 15 and one among bits 16 to 31.
All inputs are finite; a program needn't handle non-finite values. Where the computation divides by a largest or mean magnitude, that divisor is 1e-20 or more.
Results may differ from a plain program's by a relative error of at most 0.015.
Values may be sent and summed in bfloat16 or wider, within the bound.
A program may use at most 64 MiB of HBM per device.

v0:
```python
import jax
import jax.numpy as jnp
from jax import lax
from jax.sharding import PartitionSpec as P

SWEEPS = 4


ridge_scale = 0.005


def passed_along(value, axis, steps):
    count = lax.axis_size(axis)
    pairs = [(source, (source + steps) % count) for source in range(count)]
    return lax.ppermute(value, axis, pairs)


def for_sending(value):

    def short(part):
        return part.astype(jnp.bfloat16) if part.dtype == jnp.float32 else part

    return jax.tree.map(short, value)


def expand_bits(bitmaps, first_bit, bit_count, group_width):
    shifts = first_bit + jnp.arange(bit_count, dtype=jnp.int32)
    bit_values = jnp.right_shift(bitmaps[..., None], shifts) & 1
    spread = jnp.broadcast_to(bit_values[..., None], bit_values.shape + (group_width,))
    return spread.reshape(bitmaps.shape + (bit_count * group_width,)).astype(jnp.bfloat16)


def row_terms(indicator, rating_rows, factors):
    row_count = indicator.shape[0]
    rank_width = factors.shape[1]
    weighted = indicator[:, None, :] * factors.T[None, :, :]
    gram_sum = jnp.dot(
        weighted.reshape(row_count * rank_width, -1), factors, preferred_element_type=jnp.float32
    )
    gram_sum = gram_sum.reshape(row_count, rank_width, rank_width)
    right_side = jnp.dot(indicator * rating_rows, factors, preferred_element_type=jnp.float32)
    rated_count = jnp.sum(indicator.astype(jnp.float32), axis=1)
    return (gram_sum, right_side, rated_count)


def solve_rows(gram_sum, right_side, rated_count):
    rank_width = gram_sum.shape[1]
    ridge_term = ridge_scale * (rated_count + 1.0)
    identity_mat = jnp.eye(rank_width, dtype=jnp.float32)
    system = gram_sum + ridge_term[:, None, None] * identity_mat
    row_bound = jnp.max(jnp.sum(jnp.abs(system), axis=2), axis=1)
    answer = jnp.zeros_like(right_side)
    for sweep_step in range(SWEEPS):
        applied = jnp.einsum("urs,us->ur", system, answer, precision=lax.Precision.HIGHEST)
        answer = answer + (right_side - applied) / row_bound[:, None]
    return answer.astype(jnp.bfloat16)


def fetch_items(factor_shard, plan, levels):
    tiles = plan.shape[0]
    stacked = jnp.broadcast_to(factor_shard[None], (tiles,) + factor_shard.shape)
    for bit_level in range(levels):
        arrived = passed_along(stacked, "blk", -(1 << bit_level))
        selected = jnp.right_shift(plan, bit_level) & 1 == 1
        stacked = jnp.where(selected[:, None, None], arrived, stacked)
    return [stacked[k] for k in range(tiles)]


def fetch_users(factor_shard, plan, levels):
    tiles = plan.shape[0]
    whole_block = lax.all_gather(factor_shard, "grp", axis=0, tiled=True)
    stacked = jnp.broadcast_to(whole_block[None], (tiles,) + whole_block.shape)
    for bit_level in range(levels):
        arrived = passed_along(stacked, "blk", 1 << bit_level)
        selected = jnp.right_shift(plan, bit_level) & 1 == 1
        stacked = jnp.where(selected[:, None, None], arrived, stacked)
    return [stacked[k] for k in range(tiles)]


def body(item_start, ratings, rating_bits, plan):
    blocks = lax.axis_size("blk")
    groups_count = lax.axis_size("grp")
    own_half = lax.axis_index("grp")
    levels = blocks.bit_length() - 1
    group_bits = 32 // groups_count
    group_width = ratings.shape[2] // group_bits
    tiles = plan.shape[0]
    first_bit = own_half * group_bits
    indicators = expand_bits(rating_bits, first_bit, group_bits, group_width)

    def user_pass(factor_shard):
        pieces = fetch_items(factor_shard, plan, levels)
        totals = None
        for k in range(tiles):
            terms = row_terms(indicators[k], ratings[k], pieces[k])
            totals = terms if totals is None else tuple((a + b for a, b in zip(totals, terms)))
        gram_sum, right_side, rated_count = jax.tree.map(
            lambda part: part.astype(jnp.float32),
            lax.psum_scatter(for_sending(totals), "grp", scatter_dimension=0, tiled=True),
        )
        return solve_rows(gram_sum, right_side, rated_count)

    moved_ratings = ratings
    moved_bits = rating_bits
    for bit_level in range(levels):
        arrived_ratings = passed_along(moved_ratings, "blk", 1 << bit_level)
        arrived_bits = passed_along(moved_bits, "blk", 1 << bit_level)
        selected = jnp.right_shift(plan, bit_level) & 1 == 1
        moved_ratings = jnp.where(selected[:, None, None], arrived_ratings, moved_ratings)
        moved_bits = jnp.where(selected[:, None], arrived_bits, moved_bits)
    moved_indicators = expand_bits(moved_bits, first_bit, group_bits, group_width)
    first_users = user_pass(item_start)
    pieces = fetch_users(first_users, plan, levels)
    totals = None
    for k in range(tiles):
        terms = row_terms(moved_indicators[k].T, moved_ratings[k].T, pieces[k])
        totals = terms if totals is None else tuple((a + b for a, b in zip(totals, terms)))
    item_factors = solve_rows(*totals)
    user_factors = user_pass(item_factors)
    return (user_factors, item_factors)


def solution(mesh):
    in_specs = (P(("blk", "grp"), None), P(None, "blk", "grp"), P(None, "blk"), P())
    out_specs = (P(("blk", "grp"), None), P(("blk", "grp"), None))
    return jax.shard_map(body, mesh=mesh, in_specs=in_specs, out_specs=out_specs, check_vma=False)
```

profile of v0, /device:TPU:0, one launch (start us, length us, event | category | flops | bytes accessed | tf_op | source)
XLA Modules:
  0.0 249.5 jit_solution(1402965104540098551)
XLA Ops:
  10.9 5.1 %collective-permute-done = s32[4,64]{1,0:T(4,128)S(1)} collective-permute-done((s32[4,64]{1,0:T(4,128)}, s32[4,64]{1,0:T(4,128)S(1)}, u32[]{:S(2)}, u32[]{:S(2)}) %collective-permute-start) | collective-permute-done | bytes 1056 | tf_op jit(solution)/shard_map/ppermute | solution.py:15
  16.8 6.3 %collective-permute-done.1 = s32[4,64]{1,0:T(4,128)S(1)} collective-permute-done((s32[4,64]{1,0:T(4,128)S(1)}, s32[4,64]{1,0:T(4,128)S(1)}, u32[]{:S(2)}, u32[]{:S(2)}) %collective-permute-start.1) | collective-permute-done | bytes 1056 | tf_op jit(solution)/shard_map/ppermute | solution.py:15
  24.0 4.5 %collective-permute-done.2 = s32[4,64]{1,0:T(4,128)S(1)} collective-permute-done((s32[4,64]{1,0:T(4,128)S(1)}, s32[4,64]{1,0:T(4,128)S(1)}, u32[]{:S(2)}, u32[]{:S(2)}) %collective-permute-start.2) | collective-permute-done | bytes 1056 | tf_op jit(solution)/shard_map/ppermute | solution.py:15
  28.6 4.5 %collective-permute-done.3 = s32[4,64]{1,0:T(4,128)S(1)} collective-permute-done((s32[4,64]{1,0:T(4,128)S(1)}, s32[4,64]{1,0:T(4,128)S(1)}, u32[]{:S(2)}, u32[]{:S(2)}) %collective-permute-start.3) | collective-permute-done | bytes 1056 | tf_op jit(solution)/shard_map/ppermute | solution.py:15
  34.8 4.9 %collective-permute-done.9 = bf16[4,128,128]{2,1,0:T(8,128)(2,1)S(1)} collective-permute-done((bf16[4,128,128]{2,1,0:T(8,128)(2,1)S(1)}, bf16[4,128,128]{2,1,0:T(8,128)(2,1)S(1)}, u32[]{:S(2)}, u32[]{:S(2)}) %collective-permute-start.9) | collective-permute-done | bytes 131104 | tf_op jit(solution)/shard_map/ppermute | solution.py:15
  40.9 5.9 %collective-permute-done.10 = bf16[4,128,128]{2,1,0:T(8,128)(2,1)S(1)} collective-permute-done((bf16[4,128,128]{2,1,0:T(8,128)(2,1)S(1)}, bf16[4,128,128]{2,1,0:T(8,128)(2,1)S(1)}, u32[]{:S(2)}, u32[]{:S(2)}) %collective-permute-start.10) | collective-permute-done | bytes 131104 | tf_op jit(solution)/shard_map/ppermute | solution.py:15
  47.2 6.1 %collective-permute-done.11 = bf16[4,128,128]{2,1,0:T(8,128)(2,1)S(1)} collective-permute-done((bf16[4,128,128]{2,1,0:T(8,128)(2,1)S(1)}, bf16[4,128,128]{2,1,0:T(8,128)(2,1)S(1)}, u32[]{:S(2)}, u32[]{:S(2)}) %collective-permute-start.11) | collective-permute-done | bytes 131104 | tf_op jit(solution)/shard_map/ppermute | solution.py:15
  67.9 4.8 %fusion.25 = f32[32,1,128]{2,1,0:T(1,128)S(1)} fusion(f32[32,128,1]{1,2,0:T(1,128)S(1)} %bitcast.361, bf16[32,128,128]{2,1,0:T(8,128)(2,1)} %reduce-scatter.7.cloned.1.call-done, f32[128,128]{1,0:T(8,128)S(1)} %fusion.86, f32[32]{0:T(128)S(1)} %fusion.189), kind=kOutput, calls=%fused_computation.31 | convolution fusion | flops 7864320 | bytes 1147008 | tf_op jit(solution)/shard_map/urs,us->ur/dot_general | solution.py:54
  73.5 5.9 %reduce-scatter.5.cloned.1.call-done = bf16[32,128]{1,0:T(8,128)(2,1)} async-done(((bf16[64,128]{1,0:T(8,128)(2,1)}), bf16[32,128]{1,0:T(8,128)(2,1)}) %reduce-scatter.5.cloned.1.call-update) | async-done | bytes 8208 | tf_op jit(solution)/shard_map/reduce_scatter | solution.py:99
  95.3 6.2 %collective-permute-done.12 = bf16[4,64,128]{2,1,0:T(8,128)(2,1)S(1)} collective-permute-done((bf16[4,64,128]{2,1,0:T(8,128)(2,1)S(1)}, bf16[4,64,128]{2,1,0:T(8,128)(2,1)S(1)}, u32[]{:S(2)}, u32[]{:S(2)}) %collective-permute-start.12) | collective-permute-done | bytes 65568 | tf_op jit(solution)/shard_map/ppermute | solution.py:15
  103.0 5.6 %collective-permute-done.13 = bf16[4,64,128]{2,1,0:T(8,128)(2,1)S(1)} collective-permute-done((bf16[4,64,128]{2,1,0:T(8,128)(2,1)S(1)}, bf16[4,64,128]{2,1,0:T(8,128)(2,1)S(1)}, u32[]{:S(2)}, u32[]{:S(2)}) %collective-permute-start.13) | collective-permute-done | bytes 65568 | tf_op jit(solution)/shard_map/ppermute | solution.py:15
  109.9 5.6 %collective-permute-done.14 = bf16[4,64,128]{2,1,0:T(8,128)(2,1)S(1)} collective-permute-done((bf16[4,64,128]{2,1,0:T(8,128)(2,1)S(1)}, bf16[4,64,128]{2,1,0:T(8,128)(2,1)S(1)}, u32[]{:S(2)}, u32[]{:S(2)}) %collective-permute-start.14) | collective-permute-done | bytes 65568 | tf_op jit(solution)/shard_map/ppermute | solution.py:15
  127.4 5.7 %abs_reduce_fusion = (f32[128,128]{1,0:T(8,128)S(1)}, f32[128,128,128]{1,2,0:T(8,128)}) fusion(f32[128,128]{0,1:T(8,128)S(1)} %copy.89, f32[128]{0:T(128)S(1)} %add_multiply_fusion, bf16[4,64,128]{2,1,0:T(8,128)(2,1)S(1)} %get-tuple-element.34, bf16[128,64]{0,1:T(8,128)(2,1)S(1)} %get-tuple-element.10, bf16[128,64]{1,0:T(8,128)(2,1)S(1)} %get-tuple-element.26, ...), kind=kOutput, calls=%fused_computation | convolution fusion | flops 284147712 | bytes 33751552 | tf_op jit(solution)/shard_map/dot_general | solution.py:37
  133.2 10.4 %fusion.191 = f32[128,1,128]{2,1,0:T(1,128)S(1)} fusion(f32[128,128,128]{1,2,0:T(8,128)} %get-tuple-element.49, f32[128,128,1]{1,2,0:T(1,128)S(1)} %bitcast.343), kind=kOutput, calls=%fused_computation.283 | convolution fusion | flops 25165824 | bytes 8519680 | tf_op jit(solution)/shard_map/urs,us->ur/dot_general | solution.py:54
  143.9 7.2 %fusion.192 = f32[128,1,128]{2,1,0:T(1,128)S(1)} fusion(f32[128,128,128]{1,2,0:T(8,128)S(1)} %copy-done, f32[128,128,1]{1,2,0:T(1,128)S(1)} %bitcast.344), kind=kOutput, calls=%fused_computation.284 | convolution fusion | flops 25165824 | bytes 8519680 | tf_op jit(solution)/shard_map/urs,us->ur/dot_general | solution.py:54
  151.2 7.4 %fusion.193 = f32[128,1,128]{2,1,0:T(1,128)S(1)} fusion(f32[128,128,128]{1,2,0:T(8,128)S(1)} %copy-done, f32[128,128,1]{1,2,0:T(1,128)S(1)} %bitcast.341), kind=kOutput, calls=%fused_computation.285 | convolution fusion | flops 25165824 | bytes 8519680 | tf_op jit(solution)/shard_map/urs,us->ur/dot_general | solution.py:54
  158.7 7.2 %fusion.194 = f32[128,1,128]{2,1,0:T(1,128)S(1)} fusion(f32[128,128,128]{1,2,0:T(8,128)S(1)} %copy-done, f32[128,128,1]{1,2,0:T(1,128)S(1)} %bitcast.338), kind=kOutput, calls=%fused_computation.286 | convolution fusion | flops 25165824 | bytes 8519680 | tf_op jit(solution)/shard_map/urs,us->ur/dot_general | solution.py:54
  166.1 5.0 %collective-permute-done.16 = bf16[4,128,128]{2,1,0:T(8,128)(2,1)S(1)} collective-permute-done((bf16[4,128,128]{2,1,0:T(8,128)(2,1)S(1)}, bf16[4,128,128]{2,1,0:T(8,128)(2,1)S(1)}, u32[]{:S(2)}, u32[]{:S(2)}) %collective-permute-start.16) | collective-permute-done | bytes 131104 | tf_op jit(solution)/shard_map/ppermute | solution.py:15
  171.6 4.6 %collective-permute-done.17 = bf16[4,128,128]{2,1,0:T(8,128)(2,1)S(1)} collective-permute-done((bf16[4,128,128]{2,1,0:T(8,128)(2,1)S(1)}, bf16[4,128,128]{2,1,0:T(8,128)(2,1)S(1)}, u32[]{:S(2)}, u32[]{:S(2)}) %collective-permute-start.17) | collective-permute-done | bytes 131104 | tf_op jit(solution)/shard_map/ppermute | solution.py:15
  183.6 4.2 %collective-permute-done.19 = bf16[4,128,128]{2,1,0:T(8,128)(2,1)S(1)} collective-permute-done((bf16[4,128,128]{2,1,0:T(8,128)(2,1)S(1)}, bf16[4,128,128]{2,1,0:T(8,128)(2,1)S(1)}, u32[]{:S(2)}, u32[]{:S(2)}) %collective-permute-start.19) | collective-permute-done | bytes 131104 | tf_op jit(solution)/shard_map/ppermute | solution.py:15
  196.4 6.9 %add_convert_fusion = bf16[64,128,128]{2,1,0:T(8,128)(2,1)} fusion(f32[64,128,128]{2,1,0:T(8,128)} %fusion.6, f32[64,128,128]{2,1,0:T(8,128)} %fusion.10, f32[64,128,128]{2,1,0:T(8,128)} %fusion.8, bf16[128,128]{1,0:T(8,128)(2,1)S(1)} %copy.93, bf16[64,128]{1,0:T(8,128)(2,1)S(1)} %copy.80, bf16[4,128,128]{2,1,0:T(8,128)(2,1)S(1)} %broadcast_select_fusion.6), kind=kOutput, calls=%fused_computation.2 | convolution fusion | flops 273678336 | bytes 14761984 | tf_op jit(solution)/shard_map/dot_general | solution.py:37
  204.9 13.9 %reduce-scatter.11.cloned.1.call-done = bf16[32,128,128]{2,1,0:T(8,128)(2,1)} async-done(((bf16[64,128,128]{2,1,0:T(8,128)(2,1)}), bf16[32,128,128]{2,1,0:T(8,128)(2,1)}) %reduce-scatter.11.cloned.1.call-update) | async-done | bytes 1048592 | tf_op jit(solution)/shard_map/reduce_scatter | solution.py:99
  218.9 4.8 %fusion.3 = f32[32,1,128]{2,1,0:T(1,128)S(1)} fusion(f32[32,128,1]{1,2,0:T(1,128)S(1)} %bitcast.362, bf16[32,128,128]{2,1,0:T(8,128)(2,1)} %reduce-scatter.11.cloned.1.call-done, f32[128,128]{1,0:T(8,128)S(1)} %fusion.86, f32[32]{0:T(128)S(1)} %fusion.189), kind=kOutput, calls=%fused_computation.10 | convolution fusion | flops 7864320 | bytes 1147008 | tf_op jit(solution)/shard_map/urs,us->ur/dot_general | solution.py:54
  224.5 5.2 %reduce-scatter.9.cloned.1.call-done = bf16[32,128]{1,0:T(8,128)(2,1)} async-done(((bf16[64,128]{1,0:T(8,128)(2,1)}), bf16[32,128]{1,0:T(8,128)(2,1)}) %reduce-scatter.9.cloned.1.call-update) | async-done | bytes 8208 | tf_op jit(solution)/shard_map/reduce_scatter | solution.py:99
  (164 shorter events, 86.3 us)
Async XLA Ops:
  7.2 60.7 %reduce-scatter.7.cloned.1.call-start = ((), (), s32[]{:S(2)}) async-start(), calls=%async_computation.5 | async-start | bytes 3145728 | tf_op jit(solution)/shard_map/reduce_scatter | solution.py:99
  7.2 8.8 %collective-permute-start = (s32[4,64]{1,0:T(4,128)}, s32[4,64]{1,0:T(4,128)S(1)}, u32[]{:S(2)}, u32[]{:S(2)}) collective-permute-start(s32[4,64]{1,0:T(4,128)} %param.6), channel_id=1, source_target_pairs={{0,2},{2,4},{4,6},{6,8},{8,10},{10,12},{12,14},{14,16},{16,18},{18... | collective-permute-start | bytes 3080 | tf_op jit(solution)/shard_map/ppermute | solution.py:15
  16.8 6.3 %collective-permute-start.1 = (s32[4,64]{1,0:T(4,128)S(1)}, s32[4,64]{1,0:T(4,128)S(1)}, u32[]{:S(2)}, u32[]{:S(2)}) collective-permute-start(s32[4,64]{1,0:T(4,128)S(1)} %broadcast_select_fusion.16), channel_id=1, source_target_pairs={{0,4},{2,6},{4,8},{6,10},{8,12},{10,14},{12,16},{14,18},{16,20},{1... | collective-permute-start | bytes 3080 | tf_op jit(solution)/shard_map/ppermute | solution.py:15
  23.1 5.4 %collective-permute-start.2 = (s32[4,64]{1,0:T(4,128)S(1)}, s32[4,64]{1,0:T(4,128)S(1)}, u32[]{:S(2)}, u32[]{:S(2)}) collective-permute-start(s32[4,64]{1,0:T(4,128)S(1)} %broadcast_select_fusion.17), channel_id=1, source_target_pairs={{0,8},{2,10},{4,12},{6,14},{8,16},{10,18},{12,20},{14,22},{16,24},... | collective-permute-start | bytes 3080 | tf_op jit(solution)/shard_map/ppermute | solution.py:15
  23.9 10.0 %collective-permute-start.8 = (bf16[4,128,128]{2,1,0:T(8,128)(2,1)S(1)}, bf16[4,128,128]{2,1,0:T(8,128)(2,1)S(1)}, u32[]{:S(2)}, u32[]{:S(2)}) collective-permute-start(bf16[4,128,128]{2,1,0:T(8,128)(2,1)S(1)} %broadcast_in_dim.210), channel_id=1, source_target_pairs={{0,30},{2,0},{4,2},{6,4},{8,6},{10,8},{12,10},{14,12},{16,14},{18,... | collective-permute-start | bytes 393224 | tf_op jit(solution)/shard_map/ppermute | solution.py:15
  28.6 4.5 %collective-permute-start.3 = (s32[4,64]{1,0:T(4,128)S(1)}, s32[4,64]{1,0:T(4,128)S(1)}, u32[]{:S(2)}, u32[]{:S(2)}) collective-permute-start(s32[4,64]{1,0:T(4,128)S(1)} %broadcast_select_fusion.18), channel_id=1, source_target_pairs={{0,16},{2,18},{4,20},{6,22},{8,24},{10,26},{12,28},{14,30},{16,0},... | collective-permute-start | bytes 3080 | tf_op jit(solution)/shard_map/ppermute | solution.py:15
  34.7 5.0 %collective-permute-start.9 = (bf16[4,128,128]{2,1,0:T(8,128)(2,1)S(1)}, bf16[4,128,128]{2,1,0:T(8,128)(2,1)S(1)}, u32[]{:S(2)}, u32[]{:S(2)}) collective-permute-start(bf16[4,128,128]{2,1,0:T(8,128)(2,1)S(1)} %broadcast_select_fusion.1), channel_id=1, source_target_pairs={{0,28},{2,30},{4,0},{6,2},{8,4},{10,6},{12,8},{14,10},{16,12},{18,... | collective-permute-start | bytes 393224 | tf_op jit(solution)/shard_map/ppermute | solution.py:15
  40.6 6.2 %collective-permute-start.10 = (bf16[4,128,128]{2,1,0:T(8,128)(2,1)S(1)}, bf16[4,128,128]{2,1,0:T(8,128)(2,1)S(1)}, u32[]{:S(2)}, u32[]{:S(2)}) collective-permute-start(bf16[4,128,128]{2,1,0:T(8,128)(2,1)S(1)} %broadcast_select_fusion.3), channel_id=1, source_target_pairs={{0,24},{2,26},{4,28},{6,30},{8,0},{10,2},{12,4},{14,6},{16,8},{18,... | collective-permute-start | bytes 393224 | tf_op jit(solution)/shard_map/ppermute | solution.py:15
  46.9 6.3 %collective-permute-start.11 = (bf16[4,128,128]{2,1,0:T(8,128)(2,1)S(1)}, bf16[4,128,128]{2,1,0:T(8,128)(2,1)S(1)}, u32[]{:S(2)}, u32[]{:S(2)}) collective-permute-start(bf16[4,128,128]{2,1,0:T(8,128)(2,1)S(1)} %broadcast_select_fusion.5), channel_id=1, source_target_pairs={{0,16},{2,18},{4,20},{6,22},{8,24},{10,26},{12,28},{14,30},{16,0},... | collective-permute-start | bytes 393224 | tf_op jit(solution)/shard_map/ppermute | solution.py:15
  58.2 21.2 %reduce-scatter.5.cloned.1.call-start = ((), (), s32[]{:S(2)}) async-start(), calls=%async_computation.4 | async-start | bytes 24576 | tf_op jit(solution)/shard_map/reduce_scatter | solution.py:99
  59.0 36.3 %collective-permute-start.4 = (bf16[4,64,128]{2,1,0:T(8,128)(2,1)S(1)}, bf16[4,64,128]{2,1,0:T(8,128)(2,1)S(1)}, u32[]{:S(2)}, u32[]{:S(2)}) collective-permute-start(bf16[4,64,128]{2,1,0:T(8,128)(2,1)S(1)} %copy-done.4), channel_id=1, source_target_pairs={{0,2},{2,4},{4,6},{6,8},{8,10},{10,12},{12,14},{14,16},{16,18},{18... | collective-permute-start | bytes 196616 | tf_op jit(solution)/shard_map/ppermute | solution.py:15
  65.4 153.5 %reduce-scatter.11.cloned.1.call-start = ((), (), s32[]{:S(2)}) async-start(), calls=%async_computation.7 | async-start | bytes 3145728 | tf_op jit(solution)/shard_map/reduce_scatter | solution.py:99
  93.5 8.0 %collective-permute-start.12 = (bf16[4,64,128]{2,1,0:T(8,128)(2,1)S(1)}, bf16[4,64,128]{2,1,0:T(8,128)(2,1)S(1)}, u32[]{:S(2)}, u32[]{:S(2)}) collective-permute-start(bf16[4,64,128]{2,1,0:T(8,128)(2,1)S(1)} %broadcast_in_dim.214), channel_id=1, source_target_pairs={{0,2},{2,4},{4,6},{6,8},{8,10},{10,12},{12,14},{14,16},{16,18},{18... | collective-permute-start | bytes 196616 | tf_op jit(solution)/shard_map/ppermute | solution.py:15
  101.6 7.0 %collective-permute-start.13 = (bf16[4,64,128]{2,1,0:T(8,128)(2,1)S(1)}, bf16[4,64,128]{2,1,0:T(8,128)(2,1)S(1)}, u32[]{:S(2)}, u32[]{:S(2)}) collective-permute-start(bf16[4,64,128]{2,1,0:T(8,128)(2,1)S(1)} %get-tuple-element.40), channel_id=1, source_target_pairs={{0,4},{2,6},{4,8},{6,10},{8,12},{10,14},{12,16},{14,18},{16,20},{1... | collective-permute-start | bytes 196616 | tf_op jit(solution)/shard_map/ppermute | solution.py:15
  101.6 7.7 %collective-permute-start.5 = (bf16[4,64,128]{2,1,0:T(8,128)(2,1)S(1)}, bf16[4,64,128]{2,1,0:T(8,128)(2,1)S(1)}, u32[]{:S(2)}, u32[]{:S(2)}) collective-permute-start(bf16[4,64,128]{2,1,0:T(8,128)(2,1)S(1)} %get-tuple-element.41), channel_id=1, source_target_pairs={{0,4},{2,6},{4,8},{6,10},{8,12},{10,14},{12,16},{14,18},{16,20},{1... | collective-permute-start | bytes 196616 | tf_op jit(solution)/shard_map/ppermute | solution.py:15
  109.4 6.1 %collective-permute-start.14 = (bf16[4,64,128]{2,1,0:T(8,128)(2,1)S(1)}, bf16[4,64,128]{2,1,0:T(8,128)(2,1)S(1)}, u32[]{:S(2)}, u32[]{:S(2)}) collective-permute-start(bf16[4,64,128]{2,1,0:T(8,128)(2,1)S(1)} %get-tuple-element.38), channel_id=1, source_target_pairs={{0,8},{2,10},{4,12},{6,14},{8,16},{10,18},{12,20},{14,22},{16,24},... | collective-permute-start | bytes 196616 | tf_op jit(solution)/shard_map/ppermute | solution.py:15
  109.5 7.1 %collective-permute-start.6 = (bf16[4,64,128]{2,1,0:T(8,128)(2,1)S(1)}, bf16[4,64,128]{2,1,0:T(8,128)(2,1)S(1)}, u32[]{:S(2)}, u32[]{:S(2)}) collective-permute-start(bf16[4,64,128]{2,1,0:T(8,128)(2,1)S(1)} %get-tuple-element.39), channel_id=1, source_target_pairs={{0,8},{2,10},{4,12},{6,14},{8,16},{10,18},{12,20},{14,22},{16,24},... | collective-permute-start | bytes 196616 | tf_op jit(solution)/shard_map/ppermute | solution.py:15
  116.6 5.2 %collective-permute-start.15 = (bf16[4,64,128]{2,1,0:T(8,128)(2,1)S(1)}, bf16[4,64,128]{2,1,0:T(8,128)(2,1)S(1)}, u32[]{:S(2)}, u32[]{:S(2)}) collective-permute-start(bf16[4,64,128]{2,1,0:T(8,128)(2,1)S(1)} %get-tuple-element.36), channel_id=1, source_target_pairs={{0,16},{2,18},{4,20},{6,22},{8,24},{10,26},{12,28},{14,30},{16,0},... | collective-permute-start | bytes 196616 | tf_op jit(solution)/shard_map/ppermute | solution.py:15
  116.7 5.9 %collective-permute-start.7 = (bf16[4,64,128]{2,1,0:T(8,128)(2,1)S(1)}, bf16[4,64,128]{2,1,0:T(8,128)(2,1)S(1)}, u32[]{:S(2)}, u32[]{:S(2)}) collective-permute-start(bf16[4,64,128]{2,1,0:T(8,128)(2,1)S(1)} %get-tuple-element.37), channel_id=1, source_target_pairs={{0,16},{2,18},{4,20},{6,22},{8,24},{10,26},{12,28},{14,30},{16,0},... | collective-permute-start | bytes 196616 | tf_op jit(solution)/shard_map/ppermute | solution.py:15
  166.0 5.0 %collective-permute-start.16 = (bf16[4,128,128]{2,1,0:T(8,128)(2,1)S(1)}, bf16[4,128,128]{2,1,0:T(8,128)(2,1)S(1)}, u32[]{:S(2)}, u32[]{:S(2)}) collective-permute-start(bf16[4,128,128]{2,1,0:T(8,128)(2,1)S(1)} %broadcast_in_dim.219), channel_id=1, source_target_pairs={{0,30},{2,0},{4,2},{6,4},{8,6},{10,8},{12,10},{14,12},{16,14},{18,... | collective-permute-start | bytes 393224 | tf_op jit(solution)/shard_map/ppermute | solution.py:15
  171.1 5.0 %collective-permute-start.17 = (bf16[4,128,128]{2,1,0:T(8,128)(2,1)S(1)}, bf16[4,128,128]{2,1,0:T(8,128)(2,1)S(1)}, u32[]{:S(2)}, u32[]{:S(2)}) collective-permute-start(bf16[4,128,128]{2,1,0:T(8,128)(2,1)S(1)} %broadcast_select_fusion), channel_id=1, source_target_pairs={{0,28},{2,30},{4,0},{6,2},{8,4},{10,6},{12,8},{14,10},{16,12},{18,... | collective-permute-start | bytes 393224 | tf_op jit(solution)/shard_map/ppermute | solution.py:15
  176.2 5.6 %collective-permute-start.18 = (bf16[4,128,128]{2,1,0:T(8,128)(2,1)S(1)}, bf16[4,128,128]{2,1,0:T(8,128)(2,1)S(1)}, u32[]{:S(2)}, u32[]{:S(2)}) collective-permute-start(bf16[4,128,128]{2,1,0:T(8,128)(2,1)S(1)} %broadcast_select_fusion.2), channel_id=1, source_target_pairs={{0,24},{2,26},{4,28},{6,30},{8,0},{10,2},{12,4},{14,6},{16,8},{18,... | collective-permute-start | bytes 393224 | tf_op jit(solution)/shard_map/ppermute | solution.py:15
  181.9 5.9 %collective-permute-start.19 = (bf16[4,128,128]{2,1,0:T(8,128)(2,1)S(1)}, bf16[4,128,128]{2,1,0:T(8,128)(2,1)S(1)}, u32[]{:S(2)}, u32[]{:S(2)}) collective-permute-start(bf16[4,128,128]{2,1,0:T(8,128)(2,1)S(1)} %broadcast_select_fusion.4), channel_id=1, source_target_pairs={{0,16},{2,18},{4,20},{6,22},{8,24},{10,26},{12,28},{14,30},{16,0},... | collective-permute-start | bytes 393224 | tf_op jit(solution)/shard_map/ppermute | solution.py:15
  203.3 26.4 %reduce-scatter.9.cloned.1.call-start = ((), (), s32[]{:S(2)}) async-start(), calls=%async_computation.6 | async-start | bytes 24576 | tf_op jit(solution)/shard_map/reduce_scatter | solution.py:99
  (8 other events, 63.7 us)
Sparse Core Ops, SparseCore 0:
  58.3 9.4 reduce-scatter.6
  70.6 8.7 reduce-scatter.4
  203.4 15.4 reduce-scatter.10
  220.9 8.7 reduce-scatter.8
where the time goes:
time: 254 us; the launch traced here: 249 us
  waiting for transfers between devices  104 us (41%)
  matrix products  94.9 us (37%)
  between operations  15.4 us (6%)
  starting transfers between devices  14.4 us (6%)
  other arithmetic  11.6 us (5%)
  local copies, waits for them, and re-layouts  4.51 us (2%)
  blocking collectives  4.29 us (2%)
    ppermute x20, waiting for transfers between devices, passed_along(): return lax.ppermute(value, axis, pairs)  77.1 us
    dot_general x12, matrix products, solve_rows(): jnp.einsum('urs,us->ur', system, answer, precision=lax.Precision.HIGHEST)  62.5 us
    dot_general x12, matrix products, row_terms(): jnp.dot(weighted.reshape(row_count * rank_width, -1), factors, preferred_...  29 us
    reduce_scatter x4, waiting for transfers between devices, user_pass(): lax.psum_scatter(for_sending(totals), 'grp', scatter_dimension=0, tiled=T...  27.2 us
    ppermute x20, starting transfers between devices, passed_along(): return lax.ppermute(value, axis, pairs)  13.8 us
  transfers between devices with their start and end apart: 24, of which 22 were waited for; matrix products, arithmetic and copies ran while one was open for 12% of the time, Pallas kernels for 0%

commit v1 on v0

v1 whole, which is shorter than its diff:
```python
import functools

import jax
import jax.numpy as jnp
from jax import lax
from jax.experimental import pallas as pl
from jax.experimental.pallas import tpu as pltpu
from jax.sharding import PartitionSpec as P

SWEEPS = 4
WORD = 32
ridge_scale = 0.005
MESH = pl.DeviceIdType.MESH
VMEM = pl.BlockSpec(memory_space=pltpu.VMEM)
SMEM = pl.BlockSpec(memory_space=pltpu.SMEM)
F32 = jnp.float32
BF16 = jnp.bfloat16


def halves(value):
    high = value.astype(BF16)
    return high, (value - high.astype(F32)).astype(BF16)


def dot(a, b):
    return jnp.dot(a, b, preferred_element_type=F32)


def dot_nt(a, b):
    return lax.dot_general(a, b, (((1,), (1,)), ((), ())), preferred_element_type=F32)


def dot_tn(a, b):
    return lax.dot_general(a, b, (((0,), (0,)), ((), ())), preferred_element_type=F32)


def relax(factors, mask, right, count, bound):
    rows = right.shape[0]
    ridge = ridge_scale * (count + 1.0)
    inverse = 1.0 / bound
    answer = right * inverse
    for _ in range(SWEEPS - 1):
        high, low = halves(answer)
        seen = dot_nt(jnp.concatenate([high, low], axis=0), factors)
        seen = (seen[:rows] + seen[rows:]) * mask
        high, low = halves(seen)
        applied = dot(jnp.concatenate([high, low], axis=0), factors)
        applied = applied[:rows] + applied[rows:] + ridge * answer
        answer = answer + (right - applied) * inverse
    return answer.astype(BF16)


def prep_kernel(plan_ref, ratings_ref, bits_ref, bits_t_ref, send_ref, masked_ref, mask_ref):
    tiles, users, width = ratings_ref.shape
    groups = WORD // 2
    span = width // groups
    own = lax.axis_index("grp")
    half_users = users // 2
    send_ref[...] = jnp.zeros_like(send_ref)
    group_at = lax.broadcasted_iota(jnp.int32, (users, width), 1) // span + own * groups
    row_at = lax.broadcasted_iota(jnp.int32, (groups, users), 0) + own * groups
    item_at = lax.broadcasted_iota(jnp.int32, (half_users, 2 * width), 1) // span
    my_first = pl.multiple_of(own * half_users, half_users)
    for k in range(tiles):
        column = bits_t_ref[:, k:k + 1]
        shown = (jnp.right_shift(jnp.broadcast_to(column, (users, width)), group_at) & 1).astype(F32)
        masked = (ratings_ref[k].astype(F32) * shown).astype(BF16)
        masked_ref[k] = masked
        words = jnp.broadcast_to(bits_ref[k:k + 1, :], (groups, users))
        grouped = (jnp.right_shift(words, row_at) & 1).astype(F32).astype(BF16)
        offset = plan_ref[k]
        send_ref[offset, 0:users, :] = masked
        send_ref[offset, users:users + groups, 0:users] = grouped
        mine = bits_t_ref[pl.ds(my_first, half_users), k:k + 1]
        seen = jnp.right_shift(jnp.broadcast_to(mine, (half_users, 2 * width)), item_at) & 1
        mask_ref[:, k * 2 * width:(k + 1) * 2 * width] = seen.astype(F32).astype(BF16)


def gather_steps(blocks, lo, x_ref, out_ref, ssem, rsem, psem, prsem, lsem):
    me = lax.axis_index("blk")
    g = lax.axis_index("grp")
    hi = blocks // lo
    mh, ml = me // lo, me % lo
    sends = []

    def put(src, slot, device, send_sem, recv_sem):
        copy = pltpu.make_async_remote_copy(
            src_ref=src, dst_ref=out_ref.at[2 * slot + g], send_sem=send_sem, recv_sem=recv_sem,
            device_id=device, device_id_type=MESH)
        copy.start()
        sends.append(copy)

    def spread(src, slot, d):
        for e in range(1, lo):
            put(src, slot, (mh * lo + (ml + e) % lo, g), ssem.at[hi + d * lo + e], rsem.at[slot])

    def partner(src, slot, at):
        put(src, slot, (me, 1 - g), psem.at[at], prsem.at[slot])

    def arrived(slot, sem):
        pltpu.make_async_remote_copy(
            src_ref=x_ref, dst_ref=out_ref.at[2 * slot + g], send_sem=ssem.at[0], recv_sem=sem,
            device_id=(me, 1 - g), device_id_type=MESH).wait_recv()

    for d in range(1, hi):
        put(x_ref, me, (((mh + d) % hi) * lo + ml, g), ssem.at[d], rsem.at[me])
    spread(x_ref, me, 0)
    partner(x_ref, me, 0)
    local = pltpu.make_async_copy(x_ref, out_ref.at[2 * me + g], lsem)
    local.start()

    def finish():
        at = 1
        for d in range(1, hi):
            slot = ((mh + hi - d) % hi) * lo + ml
            arrived(slot, rsem.at[slot])
            spread(out_ref.at[2 * slot + g], slot, d)
            partner(out_ref.at[2 * slot + g], slot, at)
            at += 1
        for d in range(hi):
            for e in range(1, lo):
                slot = ((mh + hi - d) % hi) * lo + (ml + lo - e) % lo
                arrived(slot, rsem.at[slot])
                partner(out_ref.at[2 * slot + g], slot, at)
                at += 1
        for slot in range(blocks):
            pltpu.make_async_remote_copy(
                src_ref=x_ref, dst_ref=out_ref.at[2 * slot + 1 - g], send_sem=ssem.at[0],
                recv_sem=prsem.at[slot], device_id=(me, 1 - g), device_id_type=MESH).wait_recv()
        for copy in sends:
            copy.wait_send()
        local.wait()

    return finish


def greet_gather(blocks, lo):
    me = lax.axis_index("blk")
    g = lax.axis_index("grp")
    hi = blocks // lo
    mh, ml = me // lo, me % lo
    barrier = pltpu.get_barrier_semaphore()
    for d in range(1, hi):
        pl.semaphore_signal(barrier, inc=1, device_id=(((mh + d) % hi) * lo + ml, g), device_id_type=MESH)
    for e in range(1, lo):
        pl.semaphore_signal(barrier, inc=1, device_id=(mh * lo + (ml + e) % lo, g), device_id_type=MESH)
    pl.semaphore_signal(barrier, inc=1, device_id=(me, 1 - g), device_id_type=MESH)
    pl.semaphore_wait(barrier, hi - 1 + lo - 1 + 1)


def greet_all(blocks):
    me = lax.axis_index("blk")
    g = lax.axis_index("grp")
    barrier = pltpu.get_barrier_semaphore()
    for o in range(1, blocks):
        pl.semaphore_signal(barrier, inc=1, device_id=((me + o) % blocks, g), device_id_type=MESH)
    pl.semaphore_signal(barrier, inc=1, device_id=(me, 1 - g), device_id_type=MESH)
    pl.semaphore_wait(barrier, blocks)


def gather_kernel(blocks, lo, x_ref, out_ref, ssem, rsem, psem, prsem, lsem):
    greet_gather(blocks, lo)
    gather_steps(blocks, lo, x_ref, out_ref, ssem, rsem, psem, prsem, lsem)()


def first_kernel(blocks, lo, x_ref, send_ref, masked_ref, out_ref, slots_ref, other_ref,
                 ssem, rsem, psem, prsem, lsem, a_send, a_recv, m_send, m_recv):
    me = lax.axis_index("blk")
    g = lax.axis_index("grp")
    greet_all(blocks)
    half = other_ref.shape[1]
    finish = gather_steps(blocks, lo, x_ref, out_ref, ssem, rsem, psem, prsem, lsem)
    swap = pltpu.make_async_remote_copy(
        src_ref=masked_ref.at[:, pl.ds(pl.multiple_of((1 - g) * half, half), half), :], dst_ref=other_ref,
        send_sem=m_send, recv_sem=m_recv, device_id=(me, 1 - g), device_id_type=MESH)
    swap.start()
    moves = []
    for o in range(1, blocks):
        copy = pltpu.make_async_remote_copy(
            src_ref=send_ref.at[o], dst_ref=slots_ref.at[o], send_sem=a_send.at[o], recv_sem=a_recv.at[o],
            device_id=((me + o) % blocks, g), device_id_type=MESH)
        copy.start()
        moves.append(copy)
    finish()
    swap.wait()
    for copy in moves:
        copy.wait()


def user_kernel(blocks, plan_ref, items_ref, mask_ref, masked_ref, other_ref, out_ref, vt_ref, v_ref, sums_ref):
    me = lax.axis_index("blk")
    g = lax.axis_index("grp")
    tiles, half, width = other_ref.shape
    rank = items_ref.shape[2]
    mine = pl.multiple_of(g * half, half)
    pieces = []
    for k in range(tiles):
        source = (me + plan_ref[k]) % blocks
        for part in range(2):
            block = items_ref[2 * source + part]
            at = (2 * k + part) * width
            v_ref[at:at + width, :] = block
            vt_ref[:, at:at + width] = block.astype(F32).T.astype(BF16)
        own = masked_ref[k, pl.ds(mine, half), :].astype(F32)
        far = other_ref[k].astype(F32)
        pieces.append(jnp.where(g == 0, own, far).astype(BF16))
        pieces.append(jnp.where(g == 0, far, own).astype(BF16))
    factors = v_ref[...]
    mask = mask_ref[...].astype(F32)
    count = jnp.sum(mask, axis=1, keepdims=True)
    ridge = ridge_scale * (count + 1.0)
    right = dot(jnp.concatenate(pieces, axis=1), factors)
    diagonal = (lax.broadcasted_iota(jnp.int32, (rank, rank), 0)
                == lax.broadcasted_iota(jnp.int32, (rank, rank), 1)).astype(F32)
    turned = vt_ref[...]
    for u in range(half):
        weighted = turned * mask_ref[u:u + 1, :]
        gram = dot(weighted, factors) + ridge[u:u + 1, :] * diagonal
        sums_ref[u:u + 1, :] = jnp.sum(jnp.abs(gram), axis=0, keepdims=True)
    bound = jnp.max(sums_ref[...], axis=1, keepdims=True)
    out_ref[...] = relax(factors, mask, right, count, bound)


def item_kernel(blocks, plan_ref, users_ref, slots_ref, out_ref, mask_ref, sums_ref):
    me = lax.axis_index("blk")
    tiles = plan_ref.shape[0]
    items = out_ref.shape[0]
    rank = users_ref.shape[2]
    half = users_ref.shape[1]
    users = 2 * half
    groups = slots_ref.shape[1] - users
    span = items // groups
    factor_list, rating_list, mask_list = [], [], []
    for k in range(tiles):
        offset = plan_ref[k]
        source = (me + blocks - offset) % blocks
        factor_list += [users_ref[2 * source], users_ref[2 * source + 1]]
        rating_list.append(slots_ref[offset, 0:users, :])
        mask_list.append(slots_ref[offset, users:users + groups, 0:users].astype(F32))
    factors = jnp.concatenate(factor_list, axis=0)
    right = dot_tn(jnp.concatenate(rating_list, axis=0), factors)
    mask_ref[...] = jnp.concatenate(mask_list, axis=1)
    turned = factors.astype(F32).T.astype(BF16)
    diagonal = (lax.broadcasted_iota(jnp.int32, (rank, rank), 0)
                == lax.broadcasted_iota(jnp.int32, (rank, rank), 1)).astype(F32)
    spread = []
    for j in range(groups):
        row = mask_ref[j:j + 1, :]
        ridge = ridge_scale * (jnp.sum(row, axis=1, keepdims=True) + 1.0)
        gram = dot(turned * row.astype(BF16), factors) + ridge * diagonal
        sums_ref[j * span:(j + 1) * span, :] = jnp.broadcast_to(
            jnp.sum(jnp.abs(gram), axis=0, keepdims=True), (span, rank))
        spread.append(jnp.broadcast_to(row, (span, row.shape[1])))
    mask = jnp.concatenate(spread, axis=0)
    count = jnp.sum(mask, axis=1, keepdims=True)
    bound = jnp.max(sums_ref[...], axis=1, keepdims=True)
    out_ref[...] = relax(factors, mask, right, count, bound)


def shaped(shape, dtype=BF16):
    return jax.ShapeDtypeStruct(shape, dtype)


def gather_sems(blocks, lo):
    dma = pltpu.SemaphoreType.DMA
    hi = blocks // lo
    return [dma((hi + hi * lo,)), dma((blocks,)), dma((blocks,)), dma((blocks,)), dma(())]


def gather(value, blocks, lo, identity):
    return pl.pallas_call(
        functools.partial(gather_kernel, blocks, lo),
        out_shape=shaped((2 * blocks,) + value.shape),
        in_specs=[VMEM], out_specs=VMEM,
        scratch_shapes=gather_sems(blocks, lo),
        compiler_params=pltpu.CompilerParams(collective_id=identity, has_side_effects=True),
        name="gather_%d" % identity,
    )(value)


def body(item_start, ratings, rating_bits, plan):
    blocks = lax.axis_size("blk")
    lo = 4 if blocks % 4 == 0 else 1
    tiles, users, width = ratings.shape
    rank = item_start.shape[1]
    half = users // 2
    groups = WORD // 2
    dma = pltpu.SemaphoreType.DMA
    slot = (users + groups, width)
    send, masked, mask = pl.pallas_call(
        prep_kernel,
        out_shape=(shaped((blocks,) + slot), shaped(ratings.shape), shaped((half, tiles * 2 * width))),
        in_specs=[SMEM, VMEM, VMEM, VMEM], out_specs=(VMEM, VMEM, VMEM),
        name="prep",
    )(plan, ratings, rating_bits, rating_bits.T)
    gathered, slots, other = pl.pallas_call(
        functools.partial(first_kernel, blocks, lo),
        out_shape=(shaped((2 * blocks,) + item_start.shape), shaped((blocks,) + slot),
                   shaped((tiles, half, width))),
        in_specs=[VMEM] * 3, out_specs=(VMEM,) * 3,
        scratch_shapes=gather_sems(blocks, lo) + [dma((blocks,)), dma((blocks,)), dma(()), dma(())],
        compiler_params=pltpu.CompilerParams(collective_id=0, has_side_effects=True),
        name="first_gather",
    )(item_start, send, masked)

    def user_pass(factors):
        return pl.pallas_call(
            functools.partial(user_kernel, blocks),
            out_shape=shaped((half, rank)),
            in_specs=[SMEM] + [VMEM] * 4, out_specs=VMEM,
            scratch_shapes=[pltpu.VMEM((rank, tiles * 2 * width), BF16),
                            pltpu.VMEM((tiles * 2 * width, rank), BF16), pltpu.VMEM((half, rank), F32)],
            name="user_pass",
        )(plan, factors, mask, masked, other)

    first_users = user_pass(gathered)
    all_users = gather(first_users, blocks, lo, 1)
    item_factors = pl.pallas_call(
        functools.partial(item_kernel, blocks),
        out_shape=shaped(item_start.shape),
        in_specs=[SMEM, VMEM, VMEM], out_specs=VMEM,
        scratch_shapes=[pltpu.VMEM((groups, tiles * users), F32), pltpu.VMEM(item_start.shape, F32)],
        name="item_pass",
    )(plan, all_users, slots)
    user_factors = user_pass(gather(item_factors, blocks, lo, 2))
    return (user_factors, item_factors)


def solution(mesh):
    in_specs = (P(("blk", "grp"), None), P(None, "blk", "grp"), P(None, "blk"), P())
    out_specs = (P(("blk", "grp"), None), P(("blk", "grp"), None))
    return jax.shard_map(body, mesh=mesh, in_specs=in_specs, out_specs=out_specs, check_vma=False)
```

time: 254 us -> 66.2 us (0.26); the launches traced: 249 us -> 65.8 us
  waiting for transfers between devices: 104 us -> 0 us
  matrix products: 94.9 us -> 0 us
  Pallas kernels: 0 us -> 63.7 us
  between operations: 15.4 us -> 0.65 us
  starting transfers between devices: 14.4 us -> 0 us
  other arithmetic: 11.6 us -> 0 us
  blocking collectives: 4.29 us -> 0 us
  local copies, waits for them, and re-layouts: 4.51 us -> 1.39 us
    dot_general x36 -> x0, matrix products: 94.9 us -> none  [the longest x12 62.5 us: solve_rows(): jnp.einsum('urs,us->ur', system, answer, precision=lax.Precision.HIGHEST)]
    ppermute x20 -> x0, waiting for transfers between devices: 77.1 us -> none  [passed_along(): return lax.ppermute(value, axis, pairs)]
    pallas_call x0 -> x7, Pallas kernels: none -> 63.7 us  [the longest x2 27 us: gather(): pl.pallas_call(functools.partial(gather_kernel, blocks, lo), out_shape=sh...]
    reduce_scatter x4 -> x0, waiting for transfers between devices: 27.2 us -> none  [user_pass(): lax.psum_scatter(for_sending(totals), 'grp', scatter_dimension=0, tiled=T...]
    ppermute x20 -> x0, starting transfers between devices: 13.8 us -> none  [passed_along(): return lax.ppermute(value, axis, pairs)]
    select_n x16 -> x0, other arithmetic: 3.48 us -> none  [the longest x8 2.19 us: fetch_items(): stacked = jnp.where(selected[:, None, None], arrived, stacked)]
  transfers between devices with their start and end apart: 24 -> 0, of which waited for: 22 -> 0; matrix products, arithmetic and copies ran while one was open for 12% -> 0% of each run, Pallas kernels for 0% -> 0%
where the time goes in v1:
time: 66.2 us; the launch traced here: 65.8 us
  Pallas kernels  63.7 us (96%)
  local copies, waits for them, and re-layouts  1.39 us (2%)
    pallas_call x2, Pallas kernels, gather(): pl.pallas_call(functools.partial(gather_kernel, blocks, lo), out_shape=sh...  27 us
    pallas_call x1, Pallas kernels, body(): pl.pallas_call(functools.partial(first_kernel, blocks, lo), out_shape=(sh...  21 us
    pallas_call x2, Pallas kernels, user_pass(): pl.pallas_call(functools.partial(user_kernel, blocks), out_shape=shaped((...  10.8 us
    pallas_call x1, Pallas kernels, body(): pl.pallas_call(functools.partial(item_kernel, blocks), out_shape=shaped(i...  3.23 us
    pallas_call x1, Pallas kernels, body(): pl.pallas_call(prep_kernel, out_shape=(shaped((blocks,) + slot), shaped(r...  1.75 us
    unnamed x1, local copies, waits for them, and re-layouts  1.39 us

profile of v1, /device:TPU:0, one launch (start us, length us, event | category | flops | bytes accessed | tf_op | source)
XLA Modules:
  0.0 65.8 jit_solution(11786286322108383093)
XLA Ops:
  0.6 1.4 %copy.6 = s32[4,64]{0,1:T(8,128)} copy(s32[4,64]{1,0:T(4,128)} %bits_ref.1) | data formatting | bytes 2048 | tf_op args[2]
  2.0 1.7 %prep.1 = (bf16[16,80,128]{2,1,0:T(8,128)(2,1)}, bf16[4,64,128]{2,1,0:T(8,128)(2,1)}, bf16[32,1024]{1,0:T(8,128)(2,1)}) custom-call(s32[4]{0:T(128)} %plan_ref.7, bf16[4,64,128]{2,1,0:T(8,128)(2,1)} %ratings_ref.1, s32[4,64]{1,0:T(4,128)} %bits_ref.1, s32[64,4]{1,0:T(8,128)} %bitcast.1), custom_call_target="tpu_custom_call" | custom-call | tf_op jit(solution)/shard_map/prep/pallas_call | solution.py:290
  3.8 21.0 %first_gather.1 = (bf16[32,128,128]{2,1,0:T(8,128)(2,1)}, bf16[16,80,128]{2,1,0:T(8,128)(2,1)}, bf16[4,32,128]{2,1,0:T(8,128)(2,1)}) custom-call(bf16[128,128]{1,0:T(8,128)(2,1)} %x_ref.1, bf16[16,80,128]{2,1,0:T(8,128)(2,1)} %get-tuple-element.8.send_ref, bf16[4,64,128]{2,1,0:T(8,128)(2,1)} %get-tuple-element.9.masked_ref), custom_call_target="tpu_custom_call" | custom-call | tf_op jit(solution)/shard_map/first_gather/pallas_call | solution.py:296
  24.8 5.4 %user_pass.2.x_ref = bf16[32,128]{1,0:T(8,128)(2,1)} custom-call(s32[4]{0:T(128)} %plan_ref.7, bf16[32,128,128]{2,1,0:T(8,128)(2,1)} %get-tuple-element.10.items_ref, bf16[32,1024]{1,0:T(8,128)(2,1)} %get-tuple-element.11.mask_ref, bf16[4,64,128]{2,1,0:T(8,128)(2,1)} %get-tuple-element.9.masked_ref, bf16[4,32,128]{2,1,0:T(8,128)(2,1)} %get-tuple-element.12.other_ref), custom_call_target="tpu_custom_call" | custom-call | tf_op jit(solution)/shard_map/user_pass/pallas_call | solution.py:307
  30.1 12.7 %gather_1.1.users_ref = bf16[32,32,128]{2,1,0:T(8,128)(2,1)} custom-call(bf16[32,128]{1,0:T(8,128)(2,1)} %user_pass.2.x_ref), custom_call_target="tpu_custom_call" | custom-call | tf_op jit(solution)/shard_map/gather_1/pallas_call | solution.py:271
  42.9 3.2 %item_pass.1.x_ref = bf16[128,128]{1,0:T(8,128)(2,1)} custom-call(s32[4]{0:T(128)} %plan_ref.7, bf16[32,32,128]{2,1,0:T(8,128)(2,1)} %gather_1.1.users_ref, bf16[16,80,128]{2,1,0:T(8,128)(2,1)} %get-tuple-element.13.slots_ref), custom_call_target="tpu_custom_call" | custom-call | tf_op jit(solution)/shard_map/item_pass/pallas_call | solution.py:318
  46.1 14.3 %gather_2.1.items_ref = bf16[32,128,128]{2,1,0:T(8,128)(2,1)} custom-call(bf16[128,128]{1,0:T(8,128)(2,1)} %item_pass.1.x_ref), custom_call_target="tpu_custom_call" | custom-call | tf_op jit(solution)/shard_map/gather_2/pallas_call | solution.py:271
  60.4 5.4 %user_pass.3 = bf16[32,128]{1,0:T(8,128)(2,1)} custom-call(s32[4]{0:T(128)} %plan_ref.7, bf16[32,128,128]{2,1,0:T(8,128)(2,1)} %gather_2.1.items_ref, bf16[32,1024]{1,0:T(8,128)(2,1)} %get-tuple-element.11.mask_ref, bf16[4,64,128]{2,1,0:T(8,128)(2,1)} %get-tuple-element.9.masked_ref, bf16[4,32,128]{2,1,0:T(8,128)(2,1)} %get-tuple-element.12.other_ref), custom_call_target="tpu_custom_call" | custom-call | tf_op jit(solution)/shard_map/user_pass/pallas_call | solution.py:307

commit v2 on v1

v2 whole, which is shorter than its diff:
```python
import functools

import jax
import jax.numpy as jnp
from jax import lax
from jax.experimental import pallas as pl
from jax.experimental.pallas import tpu as pltpu
from jax.sharding import PartitionSpec as P

SWEEPS = 4
WORD = 32
ridge_scale = 0.005
MESH = pl.DeviceIdType.MESH
VMEM = pl.BlockSpec(memory_space=pltpu.VMEM)
SMEM = pl.BlockSpec(memory_space=pltpu.SMEM)
F32 = jnp.float32
BF16 = jnp.bfloat16


def halves(value):
    high = value.astype(BF16)
    return high, (value - high.astype(F32)).astype(BF16)


def dot(a, b):
    return jnp.dot(a, b, preferred_element_type=F32)


def dot_nt(a, b):
    return lax.dot_general(a, b, (((1,), (1,)), ((), ())), preferred_element_type=F32)


def dot_tn(a, b):
    return lax.dot_general(a, b, (((0,), (0,)), ((), ())), preferred_element_type=F32)


def relax(factors, mask, right, count, bound):
    rows = right.shape[0]
    ridge = ridge_scale * (count + 1.0)
    inverse = 1.0 / bound
    answer = right * inverse
    for _ in range(SWEEPS - 1):
        high, low = halves(answer)
        seen = dot_nt(jnp.concatenate([high, low], axis=0), factors)
        seen = (seen[:rows] + seen[rows:]) * mask
        high, low = halves(seen)
        applied = dot(jnp.concatenate([high, low], axis=0), factors)
        applied = applied[:rows] + applied[rows:] + ridge * answer
        answer = answer + (right - applied) * inverse
    return answer.astype(BF16)


def gather_steps(blocks, lo, x_ref, out_ref, ssem, rsem, psem, prsem, lsem):
    me = lax.axis_index("blk")
    g = lax.axis_index("grp")
    hi = blocks // lo
    mh, ml = me // lo, me % lo
    sends = []

    def put(src, slot, device, send_sem, recv_sem):
        copy = pltpu.make_async_remote_copy(
            src_ref=src, dst_ref=out_ref.at[2 * slot + g], send_sem=send_sem, recv_sem=recv_sem,
            device_id=device, device_id_type=MESH)
        copy.start()
        sends.append(copy)

    def spread(src, slot, d):
        for e in range(1, lo):
            put(src, slot, (mh * lo + (ml + e) % lo, g), ssem.at[hi + d * lo + e], rsem.at[slot])

    def partner(src, slot, at):
        put(src, slot, (me, 1 - g), psem.at[at], prsem.at[slot])

    def arrived(slot, sem):
        pltpu.make_async_remote_copy(
            src_ref=x_ref, dst_ref=out_ref.at[2 * slot + g], send_sem=ssem.at[0], recv_sem=sem,
            device_id=(me, 1 - g), device_id_type=MESH).wait_recv()

    for d in range(1, hi):
        put(x_ref, me, (((mh + d) % hi) * lo + ml, g), ssem.at[d], rsem.at[me])
    spread(x_ref, me, 0)
    partner(x_ref, me, 0)
    local = pltpu.make_async_copy(x_ref, out_ref.at[2 * me + g], lsem)
    local.start()

    def finish():
        at = 1
        for d in range(1, hi):
            slot = ((mh + hi - d) % hi) * lo + ml
            arrived(slot, rsem.at[slot])
            spread(out_ref.at[2 * slot + g], slot, d)
            partner(out_ref.at[2 * slot + g], slot, at)
            at += 1
        for d in range(hi):
            for e in range(1, lo):
                slot = ((mh + hi - d) % hi) * lo + (ml + lo - e) % lo
                arrived(slot, rsem.at[slot])
                partner(out_ref.at[2 * slot + g], slot, at)
                at += 1
        for slot in range(blocks):
            pltpu.make_async_remote_copy(
                src_ref=x_ref, dst_ref=out_ref.at[2 * slot + 1 - g], send_sem=ssem.at[0],
                recv_sem=prsem.at[slot], device_id=(me, 1 - g), device_id_type=MESH).wait_recv()
        for copy in sends:
            copy.wait_send()
        local.wait()

    return finish


def greet(blocks):
    me = lax.axis_index("blk")
    g = lax.axis_index("grp")
    barrier = pltpu.get_barrier_semaphore()
    for o in range(1, blocks):
        pl.semaphore_signal(barrier, inc=1, device_id=((me + o) % blocks, g), device_id_type=MESH)
    pl.semaphore_signal(barrier, inc=1, device_id=(me, 1 - g), device_id_type=MESH)
    return lambda: pl.semaphore_wait(barrier, blocks)


def prepare(plan_ref, ratings_ref, bits_ref, send_ref, masked_ref, mask_ref, words_ref):
    tiles, users, width = ratings_ref.shape
    groups = WORD // 2
    span = width // groups
    own = lax.axis_index("grp")
    half_users = users // 2
    words_ref[...] = jnp.zeros_like(words_ref)
    words_ref[0:tiles, 0:users] = bits_ref[...]
    words_ref[...] = words_ref[...].T
    group_at = lax.broadcasted_iota(jnp.int32, (users, width), 1) // span + own * groups
    row_at = lax.broadcasted_iota(jnp.int32, (groups, users), 0) + own * groups
    item_at = lax.broadcasted_iota(jnp.int32, (half_users, 2 * width), 1) // span
    my_first = pl.multiple_of(own * half_users, half_users)
    mine = words_ref[pl.ds(my_first, half_users), :]
    masked_list, grouped_list = [], []
    for k in range(tiles):
        column = words_ref[0:users, k:k + 1]
        shown = (jnp.right_shift(jnp.broadcast_to(column, (users, width)), group_at) & 1).astype(F32)
        masked = ratings_ref[k].astype(F32) * shown
        masked_ref[k] = masked.astype(BF16)
        masked_list.append(masked)
        words = jnp.broadcast_to(bits_ref[k:k + 1, :], (groups, users))
        grouped_list.append((jnp.right_shift(words, row_at) & 1).astype(F32))
        seen = jnp.right_shift(jnp.broadcast_to(mine[:, k:k + 1], (half_users, 2 * width)), item_at) & 1
        mask_ref[:, k * 2 * width:(k + 1) * 2 * width] = seen.astype(F32).astype(BF16)

    def fill(o, carry):
        chosen, grouped = masked_list[0], grouped_list[0]
        for k in range(1, tiles):
            chosen = jnp.where(plan_ref[k] == o, masked_list[k], chosen)
            grouped = jnp.where(plan_ref[k] == o, grouped_list[k], grouped)
        send_ref[o, 0:users, :] = chosen.astype(BF16)
        send_ref[o, users:users + groups, 0:users] = grouped.astype(BF16)
        send_ref[o, users:users + groups, users:] = jnp.zeros((groups, width - users), BF16)
        return carry

    lax.fori_loop(1, send_ref.shape[0], fill, 0)


def user_pass(blocks, plan_ref, items_ref, mask_ref, right_ref, vt_ref, v_ref, sums_ref):
    me = lax.axis_index("blk")
    half = mask_ref.shape[0]
    width, rank = items_ref.shape[1:]
    for k in range(plan_ref.shape[0]):
        source = (me + plan_ref[k]) % blocks
        for part in range(2):
            block = items_ref[2 * source + part]
            at = (2 * k + part) * width
            v_ref[at:at + width, :] = block
            vt_ref[:, at:at + width] = block.astype(F32).T.astype(BF16)
    factors = v_ref[...]
    mask = mask_ref[...].astype(F32)
    count = jnp.sum(mask, axis=1, keepdims=True)
    ridge = ridge_scale * (count + 1.0)
    right = dot(right_ref[...], factors)
    diagonal = (lax.broadcasted_iota(jnp.int32, (rank, rank), 0)
                == lax.broadcasted_iota(jnp.int32, (rank, rank), 1)).astype(F32)
    turned = vt_ref[...]
    for u in range(half):
        weighted = turned * mask_ref[u:u + 1, :]
        gram = dot(weighted, factors) + ridge[u:u + 1, :] * diagonal
        sums_ref[u:u + 1, :] = jnp.sum(jnp.abs(gram), axis=0, keepdims=True)
    bound = jnp.max(sums_ref[0:half, :], axis=1, keepdims=True)
    return relax(factors, mask, right, count, bound)


def item_pass(blocks, plan_ref, users_ref, slots_ref, mask_ref, sums_ref):
    me = lax.axis_index("blk")
    tiles = plan_ref.shape[0]
    items, rank = sums_ref.shape
    users = 2 * users_ref.shape[1]
    groups = slots_ref.shape[1] - users
    span = items // groups
    factor_list, rating_list, mask_list = [], [], []
    for k in range(tiles):
        offset = plan_ref[k]
        source = (me + blocks - offset) % blocks
        factor_list += [users_ref[2 * source], users_ref[2 * source + 1]]
        slot = slots_ref[offset]
        rating_list.append(slot[0:users])
        mask_list.append(slot[users:users + groups, 0:users].astype(F32))
    factors = jnp.concatenate(factor_list, axis=0)
    right = dot_tn(jnp.concatenate(rating_list, axis=0), factors)
    mask_ref[...] = jnp.concatenate(mask_list, axis=1)
    turned = factors.astype(F32).T.astype(BF16)
    diagonal = (lax.broadcasted_iota(jnp.int32, (rank, rank), 0)
                == lax.broadcasted_iota(jnp.int32, (rank, rank), 1)).astype(F32)
    spread = []
    for j in range(groups):
        row = mask_ref[j:j + 1, :]
        ridge = ridge_scale * (jnp.sum(row, axis=1, keepdims=True) + 1.0)
        gram = dot(turned * row.astype(BF16), factors) + ridge * diagonal
        sums_ref[j * span:(j + 1) * span, :] = jnp.broadcast_to(
            jnp.sum(jnp.abs(gram), axis=0, keepdims=True), (span, rank))
        spread.append(jnp.broadcast_to(row, (span, row.shape[1])))
    mask = jnp.concatenate(spread, axis=0)
    count = jnp.sum(mask, axis=1, keepdims=True)
    bound = jnp.max(sums_ref[...], axis=1, keepdims=True)
    return relax(factors, mask, right, count, bound)


def whole_kernel(blocks, lo, plan_ref, start_ref, ratings_ref, bits_ref, user_ref, item_ref,
                 items_ref, users_ref, again_ref, send_ref, slots_ref, masked_ref, other_ref, mask_ref,
                 right_ref, vt_ref, v_ref, sums_ref, rows_ref, words_ref, first_ref, *sems):
    me = lax.axis_index("blk")
    g = lax.axis_index("grp")
    a_send, a_recv, m_send, m_recv = sems[15:]
    tiles, half, width = other_ref.shape
    met = greet(blocks)
    prepare(plan_ref, ratings_ref, bits_ref, send_ref, masked_ref, mask_ref, words_ref)
    met()
    finish = gather_steps(blocks, lo, start_ref, items_ref, *sems[0:5])
    swap = pltpu.make_async_remote_copy(
        src_ref=masked_ref.at[:, pl.ds(pl.multiple_of((1 - g) * half, half), half), :], dst_ref=other_ref,
        send_sem=m_send, recv_sem=m_recv, device_id=(me, 1 - g), device_id_type=MESH)
    swap.start()
    finish()
    moves = []
    for o in range(1, blocks):
        copy = pltpu.make_async_remote_copy(
            src_ref=send_ref.at[o], dst_ref=slots_ref.at[o], send_sem=a_send.at[o], recv_sem=a_recv.at[o],
            device_id=((me + o) % blocks, g), device_id_type=MESH)
        copy.start()
        moves.append(copy)
    swap.wait()
    mine = pl.multiple_of(g * half, half)
    for k in range(tiles):
        own = masked_ref[k, pl.ds(mine, half), :].astype(F32)
        far = other_ref[k].astype(F32)
        at = 2 * k * width
        right_ref[:, at:at + width] = jnp.where(g == 0, own, far).astype(BF16)
        right_ref[:, at + width:at + 2 * width] = jnp.where(g == 0, far, own).astype(BF16)
    first_ref[...] = user_pass(blocks, plan_ref, items_ref, mask_ref, right_ref, vt_ref, v_ref, sums_ref)
    gather_steps(blocks, lo, first_ref, users_ref, *sems[5:10])()
    for copy in moves:
        copy.wait()
    item_ref[...] = item_pass(blocks, plan_ref, users_ref, slots_ref, rows_ref, sums_ref)
    gather_steps(blocks, lo, item_ref, again_ref, *sems[10:15])()
    user_ref[...] = user_pass(blocks, plan_ref, again_ref, mask_ref, right_ref, vt_ref, v_ref, sums_ref)


def gather_sems(blocks, lo):
    dma = pltpu.SemaphoreType.DMA
    hi = blocks // lo
    return [dma((hi + hi * lo,)), dma((blocks,)), dma((blocks,)), dma((blocks,)), dma(())]


def body(item_start, ratings, rating_bits, plan):
    blocks = lax.axis_size("blk")
    lo = 4 if blocks % 4 == 0 else 1
    tiles, users, width = ratings.shape
    items, rank = item_start.shape
    half = users // 2
    groups = WORD // 2
    dma = pltpu.SemaphoreType.DMA
    slot = (blocks, users + groups, width)
    side = tiles * 2 * width
    return pl.pallas_call(
        functools.partial(whole_kernel, blocks, lo),
        out_shape=(jax.ShapeDtypeStruct((half, rank), BF16), jax.ShapeDtypeStruct((items, rank), BF16)),
        in_specs=[SMEM] + [VMEM] * 3, out_specs=(VMEM, VMEM),
        scratch_shapes=[
            pltpu.VMEM((2 * blocks, items, rank), BF16),
            pltpu.VMEM((2 * blocks, half, rank), BF16),
            pltpu.VMEM((2 * blocks, items, rank), BF16),
            pltpu.VMEM(slot, BF16),
            pltpu.VMEM(slot, BF16),
            pltpu.VMEM((tiles, users, width), BF16),
            pltpu.VMEM((tiles, half, width), BF16),
            pltpu.VMEM((half, side), BF16),
            pltpu.VMEM((half, side), BF16),
            pltpu.VMEM((rank, side), BF16),
            pltpu.VMEM((side, rank), BF16),
            pltpu.VMEM((items, rank), F32),
            pltpu.VMEM((groups, tiles * users), F32),
            pltpu.VMEM((128, 128), jnp.int32),
            pltpu.VMEM((half, rank), BF16),
        ] + 3 * gather_sems(blocks, lo) + [dma((blocks,)), dma((blocks,)), dma(()), dma(())],
        compiler_params=pltpu.CompilerParams(collective_id=0, has_side_effects=True),
        name="sweeps",
    )(plan, item_start, ratings, rating_bits)


def solution(mesh):
    in_specs = (P(("blk", "grp"), None), P(None, "blk", "grp"), P(None, "blk"), P())
    out_specs = (P(("blk", "grp"), None), P(("blk", "grp"), None))
    return jax.shard_map(body, mesh=mesh, in_specs=in_specs, out_specs=out_specs, check_vma=False)
```

time: 66.2 us -> 53.3 us (0.81)
  Pallas kernels: 63.7 us -> 49.7 us
  local copies, waits for them, and re-layouts: 1.39 us -> 2.67 us
    pallas_call x7 -> x1, Pallas kernels: 63.7 us -> 49.7 us  [body(): pl.pallas_call(functools.partial(whole_kernel, blocks, lo), out_shape=(ja...]
    unnamed x1 -> x2, local copies, waits for them, and re-layouts: 1.39 us -> 2.67 us
where the time goes in v2:
time: 53.3 us; the launch traced here: 53 us
  Pallas kernels  49.7 us (93%)
  local copies, waits for them, and re-layouts  2.67 us (5%)
  between operations  0.64 us (1%)
    pallas_call x1, Pallas kernels, body(): pl.pallas_call(functools.partial(whole_kernel, blocks, lo), out_shape=(ja...  49.7 us
    unnamed x2, local copies, waits for them, and re-layouts  2.67 us

profile of v2, /device:TPU:0, one launch (start us, length us, event | category | flops | bytes accessed | tf_op | source)
XLA Modules:
  0.0 53.0 jit_solution(12677475845898199190)
XLA Ops:
  0.6 49.7 %sweeps.1 = (bf16[32,128]{1,0:T(8,128)(2,1)}, bf16[128,128]{1,0:T(8,128)(2,1)}) custom-call(s32[4]{0:T(128)} %plan_ref.1, bf16[128,128]{1,0:T(8,128)(2,1)} %start_ref.1, bf16[4,64,128]{2,1,0:T(8,128)(2,1)} %ratings_ref.1, s32[4,64]{1,0:T(4,128)} %bits_ref.1), custom_call_target="tpu_custom_call" | custom-call | tf_op jit(solution)/shard_map/sweeps/pallas_call | solution.py:278
  50.4 1.3 %copy.8 = bf16[32,128]{1,0:T(8,128)(2,1)} copy(bf16[32,128]{1,0:T(8,128)(2,1)} %get-tuple-element.4) | data formatting | bytes 16384
  51.7 1.4 %copy.9 = bf16[128,128]{1,0:T(8,128)(2,1)} copy(bf16[128,128]{1,0:T(8,128)(2,1)} %get-tuple-element.5) | data formatting | bytes 65536

commit v3 on v2

--- a/solution.py
+++ b/solution.py
@@ -1,4 +1,5 @@
 import functools
+import math
 
 import jax
 import jax.numpy as jnp
@@ -34,20 +35,21 @@
     return lax.dot_general(a, b, (((0,), (0,)), ((), ())), preferred_element_type=F32)
 
 
-def relax(factors, mask, right, count, bound):
-    rows = right.shape[0]
-    ridge = ridge_scale * (count + 1.0)
-    inverse = 1.0 / bound
-    answer = right * inverse
-    for _ in range(SWEEPS - 1):
-        high, low = halves(answer)
-        seen = dot_nt(jnp.concatenate([high, low], axis=0), factors)
-        seen = (seen[:rows] + seen[rows:]) * mask
-        high, low = halves(seen)
-        applied = dot(jnp.concatenate([high, low], axis=0), factors)
-        applied = applied[:rows] + applied[rows:] + ridge * answer
-        answer = answer + (right - applied) * inverse
-    return answer.astype(BF16)
+def product(factors, turned, mask, ridge, scale, vector):
+    rows = vector.shape[0]
+    seen = dot(jnp.concatenate(halves(vector), axis=0), turned)
+    seen = (seen[:rows] + seen[rows:]) * mask
+    applied = dot(jnp.concatenate(halves(seen), axis=0), factors)
+    return (applied[:rows] + applied[rows:] + ridge * vector) * scale
+
+
+def combine(powers, bound, scale):
+    inverse = 1.0 / (bound * scale)
+    total = None
+    for j in reversed(range(SWEEPS)):
+        term = powers[j] * float((-1) ** j * math.comb(SWEEPS, j + 1))
+        total = (term if total is None else term + total) * inverse
+    return (total * scale).astype(BF16)
 
 
 def gather_steps(blocks, lo, x_ref, out_ref, ssem, rsem, psem, prsem, lsem):
@@ -83,7 +85,7 @@
     local = pltpu.make_async_copy(x_ref, out_ref.at[2 * me + g], lsem)
     local.start()
 
-    def finish():
+    def finish(between=None):
         at = 1
         for d in range(1, hi):
             slot = ((mh + hi - d) % hi) * lo + ml
@@ -97,13 +99,14 @@
                 arrived(slot, rsem.at[slot])
                 partner(out_ref.at[2 * slot + g], slot, at)
                 at += 1
+        if between is not None:
+            between()
         for slot in range(blocks):
             pltpu.make_async_remote_copy(
                 src_ref=x_ref, dst_ref=out_ref.at[2 * slot + 1 - g], send_sem=ssem.at[0],
                 recv_sem=prsem.at[slot], device_id=(me, 1 - g), device_id_type=MESH).wait_recv()
-        for copy in sends:
-            copy.wait_send()
         local.wait()
+        return sends
 
     return finish
 
@@ -176,12 +179,17 @@
     diagonal = (lax.broadcasted_iota(jnp.int32, (rank, rank), 0)
                 == lax.broadcasted_iota(jnp.int32, (rank, rank), 1)).astype(F32)
     turned = vt_ref[...]
+    scale = 1.0 / (count + 1.0)
+    powers = [right]
+    segment = max(half // SWEEPS, 1)
     for u in range(half):
+        if u % segment == 0 and len(powers) < SWEEPS:
+            powers.append(product(factors, turned, mask, ridge, scale, powers[-1]))
         weighted = turned * mask_ref[u:u + 1, :]
         gram = dot(weighted, factors) + ridge[u:u + 1, :] * diagonal
         sums_ref[u:u + 1, :] = jnp.sum(jnp.abs(gram), axis=0, keepdims=True)
     bound = jnp.max(sums_ref[0:half, :], axis=1, keepdims=True)
-    return relax(factors, mask, right, count, bound)
+    return combine(powers, bound, scale)
 
 
 def item_pass(blocks, plan_ref, users_ref, slots_ref, mask_ref, sums_ref):
@@ -205,28 +213,38 @@
     turned = factors.astype(F32).T.astype(BF16)
     diagonal = (lax.broadcasted_iota(jnp.int32, (rank, rank), 0)
                 == lax.broadcasted_iota(jnp.int32, (rank, rank), 1)).astype(F32)
-    spread = []
+    mask = jnp.concatenate([jnp.broadcast_to(mask_ref[j:j + 1, :], (span, mask_ref.shape[1])) for j in range(groups)], axis=0)
+    count = jnp.sum(mask, axis=1, keepdims=True)
+    scale = 1.0 / (count + 1.0)
+    powers = [right]
+    segment = max(groups // SWEEPS, 1)
     for j in range(groups):
+        if j % segment == 0 and len(powers) < SWEEPS:
+            powers.append(product(factors, turned, mask, ridge_scale * (count + 1.0), scale, powers[-1]))
         row = mask_ref[j:j + 1, :]
         ridge = ridge_scale * (jnp.sum(row, axis=1, keepdims=True) + 1.0)
         gram = dot(turned * row.astype(BF16), factors) + ridge * diagonal
         sums_ref[j * span:(j + 1) * span, :] = jnp.broadcast_to(
             jnp.sum(jnp.abs(gram), axis=0, keepdims=True), (span, rank))
-        spread.append(jnp.broadcast_to(row, (span, row.shape[1])))
-    mask = jnp.concatenate(spread, axis=0)
-    count = jnp.sum(mask, axis=1, keepdims=True)
     bound = jnp.max(sums_ref[...], axis=1, keepdims=True)
-    return relax(factors, mask, right, count, bound)
-
-
-def whole_kernel(blocks, lo, plan_ref, start_ref, ratings_ref, bits_ref, user_ref, item_ref,
+    return combine(powers, bound, scale)
+
+
+def whole_kernel(blocks, lo, plan_ref, start_ref, ratings_hbm, bits_hbm, user_ref, item_ref,
+                 ratings_ref, bits_ref,
                  items_ref, users_ref, again_ref, send_ref, slots_ref, masked_ref, other_ref, mask_ref,
                  right_ref, vt_ref, v_ref, sums_ref, rows_ref, words_ref, first_ref, *sems):
     me = lax.axis_index("blk")
     g = lax.axis_index("grp")
-    a_send, a_recv, m_send, m_recv = sems[15:]
+    a_send, a_recv, m_send, m_recv, in_sems = sems[15:]
     tiles, half, width = other_ref.shape
     met = greet(blocks)
+    loads = [pltpu.make_async_copy(ratings_hbm, ratings_ref, in_sems.at[0]),
+             pltpu.make_async_copy(bits_hbm, bits_ref, in_sems.at[1])]
+    for load in loads:
+        load.start()
+    for load in loads:
+        load.wait()
     prepare(plan_ref, ratings_ref, bits_ref, send_ref, masked_ref, mask_ref, words_ref)
     met()
     finish = gather_steps(blocks, lo, start_ref, items_ref, *sems[0:5])
@@ -234,14 +252,17 @@
         src_ref=masked_ref.at[:, pl.ds(pl.multiple_of((1 - g) * half, half), half), :], dst_ref=other_ref,
         send_sem=m_send, recv_sem=m_recv, device_id=(me, 1 - g), device_id_type=MESH)
     swap.start()
-    finish()
     moves = []
-    for o in range(1, blocks):
-        copy = pltpu.make_async_remote_copy(
-            src_ref=send_ref.at[o], dst_ref=slots_ref.at[o], send_sem=a_send.at[o], recv_sem=a_recv.at[o],
-            device_id=((me + o) % blocks, g), device_id_type=MESH)
-        copy.start()
-        moves.append(copy)
+
+    def move():
+        for o in range(1, blocks):
+            copy = pltpu.make_async_remote_copy(
+                src_ref=send_ref.at[o], dst_ref=slots_ref.at[o], send_sem=a_send.at[o], recv_sem=a_recv.at[o],
+                device_id=((me + o) % blocks, g), device_id_type=MESH)
+            copy.start()
+            moves.append(copy)
+
+    sends = finish(move)
     swap.wait()
     mine = pl.multiple_of(g * half, half)
     for k in range(tiles):
@@ -251,12 +272,19 @@
         right_ref[:, at:at + width] = jnp.where(g == 0, own, far).astype(BF16)
         right_ref[:, at + width:at + 2 * width] = jnp.where(g == 0, far, own).astype(BF16)
     first_ref[...] = user_pass(blocks, plan_ref, items_ref, mask_ref, right_ref, vt_ref, v_ref, sums_ref)
-    gather_steps(blocks, lo, first_ref, users_ref, *sems[5:10])()
+    sends += gather_steps(blocks, lo, first_ref, users_ref, *sems[5:10])()
     for copy in moves:
-        copy.wait()
+        copy.wait_recv()
     item_ref[...] = item_pass(blocks, plan_ref, users_ref, slots_ref, rows_ref, sums_ref)
-    gather_steps(blocks, lo, item_ref, again_ref, *sems[10:15])()
+    sends += gather_steps(blocks, lo, item_ref, again_ref, *sems[10:15])()
     user_ref[...] = user_pass(blocks, plan_ref, again_ref, mask_ref, right_ref, vt_ref, v_ref, sums_ref)
+    for copy in sends + moves:
+        copy.wait_send()
+
+
+def hand_over(user_ref, item_ref, user_out, item_out):
+    user_out[...] = user_ref[...]
+    item_out[...] = item_ref[...]
 
 
 def gather_sems(blocks, lo):
@@ -275,11 +303,14 @@
     dma = pltpu.SemaphoreType.DMA
     slot = (blocks, users + groups, width)
     side = tiles * 2 * width
-    return pl.pallas_call(
+    outs = (jax.ShapeDtypeStruct((half, rank), BF16), jax.ShapeDtypeStruct((items, rank), BF16))
+    results = pl.pallas_call(
         functools.partial(whole_kernel, blocks, lo),
-        out_shape=(jax.ShapeDtypeStruct((half, rank), BF16), jax.ShapeDtypeStruct((items, rank), BF16)),
-        in_specs=[SMEM] + [VMEM] * 3, out_specs=(VMEM, VMEM),
+        out_shape=outs,
+        in_specs=[SMEM] + [pl.BlockSpec(memory_space=pl.ANY)] * 3, out_specs=(VMEM, VMEM),
         scratch_shapes=[
+            pltpu.VMEM(ratings.shape, BF16),
+            pltpu.VMEM(rating_bits.shape, jnp.int32),
             pltpu.VMEM((2 * blocks, items, rank), BF16),
             pltpu.VMEM((2 * blocks, half, rank), BF16),
             pltpu.VMEM((2 * blocks, items, rank), BF16),
@@ -295,10 +326,13 @@
             pltpu.VMEM((groups, tiles * users), F32),
             pltpu.VMEM((128, 128), jnp.int32),
             pltpu.VMEM((half, rank), BF16),
-        ] + 3 * gather_sems(blocks, lo) + [dma((blocks,)), dma((blocks,)), dma(()), dma(())],
+        ] + 3 * gather_sems(blocks, lo) + [dma((blocks,)), dma((blocks,)), dma(()), dma(()), dma((2,))],
         compiler_params=pltpu.CompilerParams(collective_id=0, has_side_effects=True),
         name="sweeps",
     )(plan, item_start, ratings, rating_bits)
+    return pl.pallas_call(
+        hand_over, out_shape=outs, in_specs=[VMEM, VMEM], out_specs=(VMEM, VMEM), name="hand_over",
+    )(*results)
 
 
 def solution(mesh):

time: 53.3 us -> 48.6 us (0.912)
  local copies, waits for them, and re-layouts: 2.67 us -> 0 us
  Pallas kernels: 49.7 us -> 47.8 us
    unnamed x2 -> x0, local copies, waits for them, and re-layouts: 2.67 us -> none
    pallas_call x1 -> x2, Pallas kernels: 49.7 us -> 47.8 us  [the longest x1 46.4 us: body(): pl.pallas_call(functools.partial(whole_kernel, blocks, lo), out_shape=out...]
where the time goes in v3:
time: 48.6 us; the launch traced here: 48.4 us
  Pallas kernels  47.8 us (98%)
  between operations  0.64 us (1%)
    pallas_call x1, Pallas kernels, body(): pl.pallas_call(functools.partial(whole_kernel, blocks, lo), out_shape=out...  46.4 us
    pallas_call x1, Pallas kernels, body(): pl.pallas_call(hand_over, out_shape=outs, in_specs=[VMEM, VMEM], out_spec...  1.4 us

profile of v3, /device:TPU:0, one launch (start us, length us, event | category | flops | bytes accessed | tf_op | source)
XLA Modules:
  0.0 48.4 jit_solution(15586131795612031637)
XLA Ops:
  0.6 46.4 %sweeps.1 = (bf16[32,128]{1,0:T(8,128)(2,1)}, bf16[128,128]{1,0:T(8,128)(2,1)}) custom-call(s32[4]{0:T(128)} %plan_ref.1, bf16[128,128]{1,0:T(8,128)(2,1)} %start_ref.1, bf16[4,64,128]{2,1,0:T(8,128)(2,1)} %ratings_hbm.1, s32[4,64]{1,0:T(4,128)} %bits_hbm.1), custom_call_target="tpu_custom_call" | custom-call | tf_op jit(solution)/shard_map/sweeps/pallas_call | solution.py:307
  47.0 1.4 %hand_over.1 = (bf16[32,128]{1,0:T(8,128)(2,1)}, bf16[128,128]{1,0:T(8,128)(2,1)}) custom-call(bf16[32,128]{1,0:T(8,128)(2,1)} %get-tuple-element.4.user_ref, bf16[128,128]{1,0:T(8,128)(2,1)} %get-tuple-element.5.item_ref), custom_call_target="tpu_custom_call" | custom-call | tf_op jit(solution)/shard_map/hand_over/pallas_call | solution.py:333

commit v4 on v3

--- a/solution.py
+++ b/solution.py
@@ -272,7 +272,7 @@
         right_ref[:, at:at + width] = jnp.where(g == 0, own, far).astype(BF16)
         right_ref[:, at + width:at + 2 * width] = jnp.where(g == 0, far, own).astype(BF16)
     first_ref[...] = user_pass(blocks, plan_ref, items_ref, mask_ref, right_ref, vt_ref, v_ref, sums_ref)
-    sends += gather_steps(blocks, lo, first_ref, users_ref, *sems[5:10])()
+    sends += gather_steps(blocks, blocks, first_ref, users_ref, *sems[5:10])()
     for copy in moves:
         copy.wait_recv()
     item_ref[...] = item_pass(blocks, plan_ref, users_ref, slots_ref, rows_ref, sums_ref)
@@ -326,7 +326,7 @@
             pltpu.VMEM((groups, tiles * users), F32),
             pltpu.VMEM((128, 128), jnp.int32),
             pltpu.VMEM((half, rank), BF16),
-        ] + 3 * gather_sems(blocks, lo) + [dma((blocks,)), dma((blocks,)), dma(()), dma(()), dma((2,))],
+        ] + gather_sems(blocks, lo) + gather_sems(blocks, blocks) + gather_sems(blocks, lo) + [dma((blocks,)), dma((blocks,)), dma(()), dma(()), dma((2,))],
         compiler_params=pltpu.CompilerParams(collective_id=0, has_side_effects=True),
         name="sweeps",
     )(plan, item_start, ratings, rating_bits)

time: 48.6 us -> 48.4 us (level)
  no operation moved by 1% of the time
where the time goes in v4:
time: 48.4 us; the launch traced here: 48.2 us
  Pallas kernels  47.5 us (98%)
  between operations  0.64 us (1%)
    pallas_call x1, Pallas kernels, body(): pl.pallas_call(functools.partial(whole_kernel, blocks, lo), out_shape=out...  46.1 us
    pallas_call x1, Pallas kernels, body(): pl.pallas_call(hand_over, out_shape=outs, in_specs=[VMEM, VMEM], out_spec...  1.4 us

profile of v4, /device:TPU:0, one launch (start us, length us, event | category | flops | bytes accessed | tf_op | source)
XLA Modules:
  0.0 48.2 jit_solution(6924913168770413593)
XLA Ops:
  0.6 46.1 %sweeps.1 = (bf16[32,128]{1,0:T(8,128)(2,1)}, bf16[128,128]{1,0:T(8,128)(2,1)}) custom-call(s32[4]{0:T(128)} %plan_ref.1, bf16[128,128]{1,0:T(8,128)(2,1)} %start_ref.1, bf16[4,64,128]{2,1,0:T(8,128)(2,1)} %ratings_hbm.1, s32[4,64]{1,0:T(4,128)} %bits_hbm.1), custom_call_target="tpu_custom_call" | custom-call | tf_op jit(solution)/shard_map/sweeps/pallas_call | solution.py:307
  46.8 1.4 %hand_over.1 = (bf16[32,128]{1,0:T(8,128)(2,1)}, bf16[128,128]{1,0:T(8,128)(2,1)}) custom-call(bf16[32,128]{1,0:T(8,128)(2,1)} %get-tuple-element.4.user_ref, bf16[128,128]{1,0:T(8,128)(2,1)} %get-tuple-element.5.item_ref), custom_call_target="tpu_custom_call" | custom-call | tf_op jit(solution)/shard_map/hand_over/pallas_call | solution.py:333
